TPU v7x, 256 devices: a whole 4x4x8 slice. The times are simulated.
256 devices in a mesh: fsdp: 64 (over x, z, core), rep: 4 (over y).
Axes of the slice: x: 4, y: 4, z: 8, core: 2. Of those that a mesh axis runs over, the one named last changes fastest.
Arguments:
- grad: bfloat16 [128, 256, 2048], P(None, 'fsdp'), may hold values from -6 to 6
- momentum: float32 [128, 256, 2048], P(None, 'fsdp'), may hold values from -6 to 6
- owner_list: int32 [128], replicated, may hold values from 0 to 63, as said below
Outputs:
- new_momentum: float32 [128, 256, 2048], P(None, 'fsdp')
- update: bfloat16 [128, 256, 2048], P(None, 'fsdp')
- owned_update: bfloat16 [256, 256, 2048], P(('fsdp', 'rep'))
Inputs may be any that keep to these rules, and one draw needn't show every extreme that they name: `owner_list`: no owner is named by more than 4 matrices; some owner is named by exactly 4 in every draw.
All inputs are finite; a program needn't handle non-finite values.
Results may differ from a plain program's by a relative error of at most 0.03.
Values may be sent and summed in bfloat16 or wider, within the bound.
A program may use at most 128 MiB of HBM per device.

v0:
```python
import jax
import jax.numpy as jnp
from jax import lax
from jax.sharding import PartitionSpec as P

CAP = 4
ITERS = 5
decay_rate = 0.95
norm_eps = 1e-07
quintic_a = 3.4445
quintic_b = -4.775
quintic_c = 2.0315


def newton(blended):
    values = blended.astype(jnp.float32)
    total = jnp.sqrt(jnp.sum(values * values))
    current = (values / (total + norm_eps)).astype(jnp.bfloat16)
    for iteration in range(ITERS):
        gram = jnp.dot(current, current.T, preferred_element_type=jnp.float32).astype(jnp.bfloat16)
        square = jnp.dot(gram, gram, preferred_element_type=jnp.float32)
        poly = (quintic_b * gram.astype(jnp.float32) + quintic_c * square).astype(jnp.bfloat16)
        applied = jnp.dot(poly, current, preferred_element_type=jnp.float32)
        current = (quintic_a * current.astype(jnp.float32) + applied).astype(jnp.bfloat16)
    return current


def local(grad, momentum, owner_list):
    matrix_count, row_count, col_count = grad.shape
    owner_count = lax.axis_size("fsdp")
    replicas = lax.axis_size("rep")
    capacity = CAP
    per_replica = capacity // replicas
    replica = lax.axis_index("rep")
    new_momentum = decay_rate * momentum + grad.astype(jnp.float32)
    blended = (grad.astype(jnp.float32) + decay_rate * new_momentum).astype(jnp.bfloat16)
    order = jnp.arange(matrix_count)
    earlier = order[None, :] < order[:, None]
    same_owner = owner_list[None, :] == owner_list[:, None]
    slot_index = jnp.sum(jnp.logical_and(earlier, same_owner), axis=1)
    position = slot_index * owner_count + owner_list
    targets = jnp.arange(capacity * owner_count)
    matched = position[None, :] == targets[:, None]
    sources = jnp.sum(jnp.where(matched, order[None, :], 0), axis=1)
    filled = jnp.any(matched, axis=1)
    flattened = blended.reshape(matrix_count, row_count * col_count)
    first_slot = replica * per_replica
    chosen = lax.dynamic_slice_in_dim(sources, first_slot * owner_count, per_replica * owner_count)
    usable = lax.dynamic_slice_in_dim(filled, first_slot * owner_count, per_replica * owner_count)
    picked = jnp.take(flattened, chosen, axis=0)
    picked = jnp.where(usable[:, None], picked, jnp.zeros_like(picked))
    outgoing = picked.reshape(per_replica, owner_count, row_count, col_count)
    received = lax.all_to_all(outgoing, "fsdp", split_axis=1, concat_axis=1, tiled=True)
    items = received.shape[0]
    matrices = received.reshape(items, owner_count * row_count, col_count)
    result = jax.vmap(newton)(matrices)
    finished = result.reshape(items, owner_count, row_count, col_count)
    owned_update = finished.reshape(per_replica, owner_count * row_count, col_count)
    returned = lax.all_to_all(finished, "fsdp", split_axis=1, concat_axis=1, tiled=True)
    complete = lax.all_gather(returned, "rep", axis=0, tiled=True)
    stacked = complete.reshape(capacity * owner_count, row_count, col_count)
    update = jnp.take(stacked, position, axis=0)
    return (new_momentum, update, owned_update)


def solution(mesh):
    in_specs = (P(None, "fsdp", None), P(None, "fsdp", None), P())
    out_specs = (P(None, "fsdp", None), P(None, "fsdp", None), P(("fsdp", "rep"), None, None))
    return jax.shard_map(local, mesh=mesh, in_specs=in_specs, out_specs=out_specs, check_vma=False)
```

profile of v0, /device:TPU:1, one launch (start us, length us, event | category | flops | bytes accessed | tf_op | source)
XLA Modules:
  0.0 174.7 jit_solution(12986220659537661177)
XLA Ops:
  7.2 0.0 all-gather.2.cloned.1.call-start
  7.2 0.9 convert_reduce_fusion
  8.1 0.7 compare_and_fusion.1
  8.8 0.1 select_reduce_fusion
  8.9 0.1 fusion.39
  9.0 5.5 %fusion = (bf16[128,4,2048]{2,1,0:T(4,128)(2,1)S(1)}, f32[128,4,2048]{2,1,0:T(4,128)}) fusion(bf16[128,4,2048]{2,1,0:T(4,128)(2,1)} %param.3, f32[128,4,2048]{2,1,0:T(4,128)} %param.4), kind=kLoop, calls=%fused_computation.4 | loop fusion | flops 6291456 | bytes 12582912 | tf_op jit(solution)/shard_map/convert_element_type | solution.py:36
  14.6 1.4 copy.14
  16.0 0.1 compare_and_fusion
  16.1 1.2 gather_fusion
  17.3 0.8 gather.11
  18.1 0.1 dynamic_slice.6
  18.2 0.7 fusion.18
  18.9 41.3 %all_to_all.10 = bf16[1,64,4,2048]{3,2,0,1:T(4,128)(2,1)S(1)} all-to-all(bf16[1,64,4,2048]{3,2,0,1:T(4,128)(2,1)S(1)} %fusion.18), channel_id=1, replica_groups=mesh['fsdp'=64,'rep'=4] {'fsdp'}, dimensions={1} | all-to-all | bytes 2097152 | tf_op jit(solution)/shard_map/all_to_all | solution.py:53
  60.2 1.7 fusion.6
  62.6 0.6 fusion.7
  63.2 0.3 convert_element_type.146
  63.5 0.5 convolution_convert_fusion.4
  64.0 0.6 fusion.1
  64.6 0.5 convolution_convert_fusion.3
  65.0 0.6 fusion.2
  65.6 0.5 convolution_convert_fusion.2
  66.1 0.6 fusion.3
  66.7 0.5 convolution_convert_fusion.1
  67.2 0.6 fusion.4
  67.7 0.5 convolution_convert_fusion
  68.2 0.6 fusion.5
  68.8 0.0 copy-start
  68.8 0.4 reshape.205
  69.3 34.7 %all_to_all.11 = bf16[1,64,4,2048]{3,2,0,1:T(4,128)(2,1)S(1)} all-to-all(bf16[1,64,4,2048]{3,2,0,1:T(4,128)(2,1)S(1)} %bitcast.39), channel_id=1, replica_groups=mesh['fsdp'=64,'rep'=4] {'fsdp'}, dimensions={1} | all-to-all | bytes 2097152 | tf_op jit(solution)/shard_map/all_to_all | solution.py:59
  104.0 0.0 copy-done
  104.0 1.5 copy.12
  105.5 0.0 all-gather.2.cloned.1.call-update
  105.6 48.0 %all-gather.2.cloned.1.call-done = bf16[4,64,4,2048]{3,1,2,0:T(8,128)(2,1)} async-done(((bf16[1,64,4,2048]{3,1,2,0:T(8,128)(2,1)}), bf16[4,64,4,2048]{3,1,2,0:T(8,128)(2,1)}) %all-gather.2.cloned.1.call-update) | async-done | bytes 4194320 | tf_op jit(solution)/shard_map/all_gather | solution.py:60
  153.6 7.4 %copy.13 = bf16[4,64,4,2048]{3,2,1,0:T(4,128)(2,1)} copy(bf16[4,64,4,2048]{3,1,2,0:T(8,128)(2,1)} %all-gather.2.cloned.1.call-done) | data formatting | bytes 8388608 | tf_op jit(solution)/shard_map/all_gather | solution.py:60
  161.0 4.5 %gather_fusion.1 = bf16[128,4,2048]{2,1,0:T(4,128)(2,1)S(1)} fusion(bf16[256,4,2048]{2,1,0:T(4,128)(2,1)} %bitcast.37, s32[1024]{0:T(1024)S(1)} %pad_clamp_fusion), kind=kCustom, calls=%fused_computation.1 | custom fusion | bytes 4194816 | tf_op jit(solution)/shard_map/jit(_take)/gather | solution.py:62
  165.5 2.4 %broadcast_select_fusion = bf16[128,4,2048]{2,1,0:T(4,128)(2,1)} fusion(bf16[128,4,2048]{2,1,0:T(4,128)(2,1)S(1)} %gather_fusion.1, pred[128]{0:T(512)(128)(4,1)S(1)} %get-tuple-element.3), kind=kLoop, calls=%fused_computation.19 | loop fusion | flops 1048576 | bytes 4194432 | tf_op jit(solution)/shard_map/jit(_take)/select_n | solution.py:62
  (3 shorter events, 0.0 us)
Async XLA Ops:
  7.2 146.4 %all-gather.2.cloned.1.call-start = ((), (), s32[]{:S(2)}) async-start(), calls=%async_computation.2 | async-start | bytes 5242880 | tf_op jit(solution)/shard_map/all_gather | solution.py:60
  68.8 35.2 %copy-start = (bf16[256,2048]{1,0:T(8,128)(2,1)}, bf16[256,2048]{1,0:T(8,128)(2,1)S(1)}, u32[]{:S(2)}) copy-start(bf16[256,2048]{1,0:T(8,128)(2,1)S(1)} %fusion.5) | copy-start | bytes 3145732
Sparse Core Ops, SparseCore 0:
  105.7 47.8 all-gather.1
where the time goes:
time: 175 us
  blocking collectives  76.1 us (43%)
  waiting for transfers between devices  48 us (27%)
  local copies, waits for them, and re-layouts  17.7 us (10%)
  between operations  14.9 us (9%)
  other arithmetic  12.8 us (7%)
  matrix products  5.23 us (3%)
    all_gather x1, waiting for transfers between devices, local(): complete = lax.all_gather(returned, 'rep', axis=0, tiled=True)  48 us
    all_to_all x1, blocking collectives, local(): lax.all_to_all(outgoing, 'fsdp', split_axis=1, concat_axis=1, tiled=True)  41.3 us
    all_to_all x1, blocking collectives, local(): lax.all_to_all(finished, 'fsdp', split_axis=1, concat_axis=1, tiled=True)  34.7 us
    all_gather x1, local copies, waits for them, and re-layouts, local(): complete = lax.all_gather(returned, 'rep', axis=0, tiled=True)  7.43 us
    convert_element_type x1, other arithmetic, local(): (grad.astype(jnp.float32) + decay_rate * new_momentum).astype(jnp.bfloat16)  5.54 us
    gather x1, local copies, waits for them, and re-layouts, local(): update = jnp.take(stacked, position, axis=0)  4.52 us
  transfers between devices with their start and end apart: 1, of which 1 were waited for; matrix products, arithmetic and copies ran while one was open for 0% of the time, Pallas kernels for 0%

commit v1 on v0

--- a/solution.py
+++ b/solution.py
@@ -10,6 +10,12 @@
 quintic_a = 3.4445
 quintic_b = -4.775
 quintic_c = 2.0315
+
+
+def in_order(blocks, dim):
+    blocks = jnp.moveaxis(blocks, 0, dim)
+    shape = blocks.shape
+    return blocks.reshape(*shape[:dim], shape[dim] * shape[dim + 1], *shape[dim + 2 :])
 
 
 def newton(blended):
@@ -57,7 +63,19 @@
     finished = result.reshape(items, owner_count, row_count, col_count)
     owned_update = finished.reshape(per_replica, owner_count * row_count, col_count)
     returned = lax.all_to_all(finished, "fsdp", split_axis=1, concat_axis=1, tiled=True)
-    complete = lax.all_gather(returned, "rep", axis=0, tiled=True)
+    length = lax.axis_size("rep")
+    pairs = [(i, (i + 1) % length) for i in range(length)]
+    back = [(b, a) for a, b in pairs]
+    lower, upper = ([], [])
+    for step in range(length - 1):
+        if step % 2 == 0:
+            lower.append(lax.ppermute(lower[-1] if lower else returned, "rep", pairs))
+        else:
+            upper.append(lax.ppermute(upper[-1] if upper else returned, "rep", back))
+    parts = jnp.stack([*lower[::-1], returned, *upper])
+    shift = lax.axis_index("rep") - len(lower)
+    parts = parts[(jnp.arange(length) - shift) % length]
+    complete = in_order(parts, 0)
     stacked = complete.reshape(capacity * owner_count, row_count, col_count)
     update = jnp.take(stacked, position, axis=0)
     return (new_momentum, update, owned_update)

time: 175 us -> 169 us (0.966)
  between operations: 14.9 us -> 1.52 us
  other arithmetic: 12.8 us -> 18.8 us
  starting transfers between devices: 0.04 us -> 2.73 us
    ppermute x0 -> x3, waiting for transfers between devices: none -> 48.4 us  [the longest x2 48.4 us: local(): lower.append(lax.ppermute(lower[-1] if lower else returned, 'rep', pairs))]
    all_gather x1 -> x0, waiting for transfers between devices: 48 us -> none  [local(): complete = lax.all_gather(returned, 'rep', axis=0, tiled=True)]
    gather x0 -> x1, local copies, waits for them, and re-layouts: none -> 7.52 us  [local(): parts = parts[(jnp.arange(length) - shift) % length]]
    all_gather x1 -> x0, local copies, waits for them, and re-layouts: 7.43 us -> none  [local(): complete = lax.all_gather(returned, 'rep', axis=0, tiled=True)]
    another operation x0 -> x1, other arithmetic: none -> 5.98 us  [local(): parts = jnp.stack([*lower[::-1], returned, *upper])]
    ppermute x0 -> x3, starting transfers between devices: none -> 2.73 us  [the longest x1 1.43 us: local(): upper.append(lax.ppermute(upper[-1] if upper else returned, 'rep', back))]
  transfers between devices with their start and end apart: 1 -> 3, of which waited for: 1 -> 2; matrix products, arithmetic and copies ran while one was open for 0% -> 0% of each run, Pallas kernels for 0% -> 0%
where the time goes in v1:
time: 169 us
  blocking collectives  76.1 us (45%)
  waiting for transfers between devices  48.4 us (29%)
  other arithmetic  18.8 us (11%)
  local copies, waits for them, and re-layouts  16.3 us (10%)
  matrix products  5.23 us (3%)
  starting transfers between devices  2.73 us (2%)
    ppermute x2, waiting for transfers between devices, local(): lower.append(lax.ppermute(lower[-1] if lower else returned, 'rep', pairs))  48.4 us
    all_to_all x1, blocking collectives, local(): lax.all_to_all(outgoing, 'fsdp', split_axis=1, concat_axis=1, tiled=True)  41.3 us
    all_to_all x1, blocking collectives, local(): lax.all_to_all(finished, 'fsdp', split_axis=1, concat_axis=1, tiled=True)  34.7 us
    gather x1, local copies, waits for them, and re-layouts, local(): parts = parts[(jnp.arange(length) - shift) % length]  7.52 us
    another operation x1, other arithmetic, local(): parts = jnp.stack([*lower[::-1], returned, *upper])  5.98 us
    convert_element_type x1, other arithmetic, local(): (grad.astype(jnp.float32) + decay_rate * new_momentum).astype(jnp.bfloat16)  5.54 us
    gather x1, local copies, waits for them, and re-layouts, local(): update = jnp.take(stacked, position, axis=0)  4.52 us
  transfers between devices with their start and end apart: 3, of which 2 were waited for; matrix products, arithmetic and copies ran while one was open for 0% of the time, Pallas kernels for 0%

profile of v1, /device:TPU:1, one launch (start us, length us, event | category | flops | bytes accessed | tf_op | source)
XLA Modules:
  0.0 169.0 jit_solution(10908245870579613609)
XLA Ops:
  0.6 0.9 convert_reduce_fusion
  1.5 0.7 compare_and_fusion.1
  2.2 0.1 select_reduce_fusion
  2.3 0.1 fusion.39
  2.4 5.5 %fusion = (bf16[128,4,2048]{2,1,0:T(4,128)(2,1)S(1)}, f32[128,4,2048]{2,1,0:T(4,128)}) fusion(bf16[128,4,2048]{2,1,0:T(4,128)(2,1)} %param.3, f32[128,4,2048]{2,1,0:T(4,128)} %param.4), kind=kLoop, calls=%fused_computation.5 | loop fusion | flops 6291456 | bytes 12582912 | tf_op jit(solution)/shard_map/convert_element_type | solution.py:42
  8.0 1.4 copy.12
  9.4 0.1 compare_and_fusion
  9.5 1.2 gather_fusion
  10.7 0.8 gather.14
  11.5 0.1 dynamic_slice.6
  11.6 0.7 fusion.18
  12.3 41.3 %all_to_all.10 = bf16[1,64,4,2048]{3,2,0,1:T(4,128)(2,1)S(1)} all-to-all(bf16[1,64,4,2048]{3,2,0,1:T(4,128)(2,1)S(1)} %fusion.18), channel_id=1, replica_groups=mesh['fsdp'=64,'rep'=4] {'fsdp'}, dimensions={1} | all-to-all | bytes 2097152 | tf_op jit(solution)/shard_map/all_to_all | solution.py:59
  53.7 1.7 fusion.6
  56.0 0.6 fusion.7
  56.6 0.3 convert_element_type.146
  56.9 0.5 convolution_convert_fusion.4
  57.4 0.6 fusion.1
  58.0 0.5 convolution_convert_fusion.3
  58.5 0.6 fusion.2
  59.0 0.5 convolution_convert_fusion.2
  59.5 0.6 fusion.3
  60.1 0.5 convolution_convert_fusion.1
  60.6 0.6 fusion.4
  61.2 0.5 convolution_convert_fusion
  61.6 0.6 fusion.5
  62.2 0.0 copy-start
  62.2 0.4 reshape.251
  62.7 34.7 %all_to_all.11 = bf16[1,64,4,2048]{3,2,0,1:T(4,128)(2,1)S(1)} all-to-all(bf16[1,64,4,2048]{3,2,0,1:T(4,128)(2,1)S(1)} %bitcast.48), channel_id=1, replica_groups=mesh['fsdp'=64,'rep'=4] {'fsdp'}, dimensions={1} | all-to-all | bytes 2097152 | tf_op jit(solution)/shard_map/all_to_all | solution.py:65
  97.4 0.0 copy-done
  97.4 1.3 collective-permute-start
  98.7 1.4 collective-permute-start.2
  100.1 23.3 %collective-permute-done = bf16[1,64,4,2048]{3,2,1,0:T(4,128)(2,1)S(1)} collective-permute-done((bf16[1,64,4,2048]{3,2,1,0:T(4,128)(2,1)S(1)}, bf16[1,64,4,2048]{3,2,1,0:T(4,128)(2,1)S(1)}, u32[]{:S(2)}, u32[]{:S(2)}) %collective-permute-start) | collective-permute-done | bytes 1048608 | tf_op jit(solution)/shard_map/ppermute | solution.py:72
  123.4 0.0 collective-permute-start.1
  123.5 0.0 collective-permute-done.2
  123.5 25.1 %collective-permute-done.1 = bf16[1,64,4,2048]{3,2,1,0:T(4,128)(2,1)} collective-permute-done((bf16[1,64,4,2048]{3,2,1,0:T(4,128)(2,1)S(1)}, bf16[1,64,4,2048]{3,2,1,0:T(4,128)(2,1)}, u32[]{:S(2)}, u32[]{:S(2)}) %collective-permute-start.1) | collective-permute-done | bytes 1048608 | tf_op jit(solution)/shard_map/ppermute | solution.py:72
  148.6 6.0 %maximum_bitcast_fusion = bf16[4,64,4,2048]{3,2,1,0:T(4,128)(2,1)} fusion(bf16[1,1,64,4,2048]{4,3,2,1,0:T(4,128)(2,1)S(1)} %bitcast.53, bf16[1,1,64,4,2048]{4,3,2,1,0:T(4,128)(2,1)S(1)} %bitcast.50, bf16[1,1,64,4,2048]{4,3,2,1,0:T(4,128)(2,1)S(1)} %bitcast.52, bf16[1,1,64,4,2048]{4,3,2,1,0:T(4,128)(2,1)} %bitcast.3), kind=kLoop, calls=%fused_computation.6 | loop fusion | flops 6291456 | bytes 8388608 | tf_op jit(solution)/shard_map/stack | solution.py:75
  154.6 7.5 %gather_fusion.1 = bf16[4,64,4,2048]{3,2,1,0:T(4,128)(2,1)} fusion(bf16[4,64,4,2048]{3,2,1,0:T(4,128)(2,1)} %maximum_bitcast_fusion, s32[1024]{0:T(1024)S(1)} %pad_clamp_fusion.1), kind=kCustom, calls=%fused_computation.1 | custom fusion | bytes 8388624 | tf_op jit(solution)/shard_map/gather | solution.py:77
  162.1 4.5 %gather_fusion.2 = bf16[128,4,2048]{2,1,0:T(4,128)(2,1)S(1)} fusion(bf16[256,4,2048]{2,1,0:T(4,128)(2,1)} %bitcast.46, s32[1024]{0:T(1024)S(1)} %pad_clamp_fusion), kind=kCustom, calls=%fused_computation.2 | custom fusion | bytes 4194816 | tf_op jit(solution)/shard_map/jit(_take)/gather | solution.py:80
  166.6 2.4 %broadcast_select_fusion = bf16[128,4,2048]{2,1,0:T(4,128)(2,1)} fusion(bf16[128,4,2048]{2,1,0:T(4,128)(2,1)S(1)} %gather_fusion.2, pred[128]{0:T(512)(128)(4,1)S(1)} %get-tuple-element.3), kind=kLoop, calls=%fused_computation.21 | loop fusion | flops 1048576 | bytes 4194432 | tf_op jit(solution)/shard_map/jit(_take)/select_n | solution.py:80
  (5 shorter events, 0.0 us)
Async XLA Ops:
  62.2 35.2 %copy-start = (bf16[256,2048]{1,0:T(8,128)(2,1)}, bf16[256,2048]{1,0:T(8,128)(2,1)S(1)}, u32[]{:S(2)}) copy-start(bf16[256,2048]{1,0:T(8,128)(2,1)S(1)} %fusion.5) | copy-start | bytes 3145732
  97.4 26.0 %collective-permute-start = (bf16[1,64,4,2048]{3,2,1,0:T(4,128)(2,1)S(1)}, bf16[1,64,4,2048]{3,2,1,0:T(4,128)(2,1)S(1)}, u32[]{:S(2)}, u32[]{:S(2)}) collective-permute-start(bf16[1,64,4,2048]{3,2,1,0:T(4,128)(2,1)S(1)} %bitcast.49), channel_id=1, source_target_pairs={{0,1},{1,2},{2,3},{3,0},{4,5},{5,6},{6,7},{7,4},{8,9},{9,10},{10,1... | collective-permute-start | bytes 3145736 | tf_op jit(solution)/shard_map/ppermute | solution.py:72
  98.7 24.8 %collective-permute-start.2 = (bf16[1,64,4,2048]{3,2,0,1:T(4,128)(2,1)S(1)}, bf16[1,64,4,2048]{3,2,0,1:T(4,128)(2,1)S(1)}, u32[]{:S(2)}, u32[]{:S(2)}) collective-permute-start(bf16[1,64,4,2048]{3,2,0,1:T(4,128)(2,1)S(1)} %all_to_all.11), channel_id=1, source_target_pairs={{1,0},{2,1},{3,2},{0,3},{5,4},{6,5},{7,6},{4,7},{9,8},{10,9},{11,1... | collective-permute-start | bytes 3145736 | tf_op jit(solution)/shard_map/ppermute | solution.py:74
  123.4 25.2 %collective-permute-start.1 = (bf16[1,64,4,2048]{3,2,1,0:T(4,128)(2,1)S(1)}, bf16[1,64,4,2048]{3,2,1,0:T(4,128)(2,1)}, u32[]{:S(2)}, u32[]{:S(2)}) collective-permute-start(bf16[1,64,4,2048]{3,2,1,0:T(4,128)(2,1)S(1)} %collective-permute-done), channel_id=1, source_target_pairs={{0,1},{1,2},{2,3},{3,0},{4,5},{5,6},{6,7},{7,4},{8,9},{9,10},{10,1... | collective-permute-start | bytes 3145736 | tf_op jit(solution)/shard_map/ppermute | solution.py:72
